TPU v7x, 128 devices: a whole 4x4x4 slice. The times are simulated.
128 devices in a mesh: group: 8 (over x_lo, z), tensor: 16 (over x_hi, y, core).
Axes of the slice: x: 4 (x_hi: 2, x_lo: 2; x = x_hi * 2 + x_lo), y: 4, z: 4, core: 2. Of those that a mesh axis runs over, the one named last changes fastest.
Arguments:
- hidden: bfloat16 [12288, 2048], P(('group', 'tensor')), may hold values from -20 to 20
- request_of: int32 [12288], P('group'), may hold values from 0 to 191, as said below
- positions: int32 [12288], P('group'), may hold values from 0 to 511, as said below
- page_table: int32 [8, 64], P('group'), may hold values from 0 to 63, each once within a row
- attn_gain: float32 [2048], replicated, may hold values from 0.5 to 1.5
- mlp_gain: float32 [2048], replicated, may hold values from 0.5 to 1.5
- wq: float32 [2048, 2048], P('group', 'tensor'), may hold values from -2 to 2
- wk: float32 [2048, 1024], P('group', 'tensor'), may hold values from -1 to 1
- wv: float32 [2048, 1024], P('group', 'tensor'), may hold values from -0.125 to 0.125
- wo: float32 [2048, 2048], P('tensor', 'group'), may hold values from -0.125 to 0.125
- w_gate: float32 [2048, 8192], P('group', 'tensor'), may hold values from -0.125 to 0.125
- w_up: float32 [2048, 8192], P('group', 'tensor'), may hold values from -0.125 to 0.125
- w_down: float32 [8192, 2048], P('tensor', 'group'), may hold values from -0.0625 to 0.0625
Outputs:
- layer_out: bfloat16 [12288, 2048], P(('group', 'tensor'))
- kv_pages: bfloat16 [512, 128, 2048], P('group', None, 'tensor')
Inputs may be any that keep to these rules, and one draw needn't show every extreme that they name: `request_of`: prompt numbers rise strictly along the token stream, starting at 0, and the last prompt of the stream has the number 12288 // 64 - 1; a prompt's rows are consecutive, and a prompt that reaches the last row of one block of 1536 rows continues at the first row of the next block. A prompt's rows have positions 0, 1, 2 and so on in order; a prompt has at most 512 rows, and one has exactly 512.
All inputs are finite; a program needn't handle non-finite values.
Results may differ from a plain program's by a relative error of at most 0.014.
Values may be sent and summed in bfloat16 or wider, within the bound.
A program may use at most 128 MiB of HBM per device.

v0:
```python
import jax
import jax.numpy as jnp
from jax import lax
from jax.sharding import PartitionSpec as P

QH = 16
KVH = 8
HD = 128
PAGE = 128
rope_base = 1000000.0
norm_eps = 1e-06


def partner(value, axis, distance):
    mask = 2**distance
    pairs = [(source, source ^ mask) for source in range(lax.axis_size(axis))]
    return lax.ppermute(value, axis, pairs)


def from_behind(block, axis, distance):
    devices = range(lax.axis_size(axis))
    route = [(i - distance, i) for i in devices if i - distance in devices]
    return lax.ppermute(block, axis, route)


def rms_scale(values, gain):
    square = jnp.mean(values * values, axis=-1, keepdims=True)
    return (values * lax.rsqrt(square + norm_eps) * gain).astype(jnp.bfloat16)


def rotate(values, places):
    half_dim = values.shape[-1] // 2
    frequency = rope_base ** (-(jnp.arange(half_dim, dtype=jnp.float32) * 2.0 / values.shape[-1]))
    angle = places.astype(jnp.float32)[:, None] * frequency[None, :]
    cosine = jnp.cos(angle)[:, None, :]
    sine = jnp.sin(angle)[:, None, :]
    widened = values.astype(jnp.float32)
    first = widened[..., :half_dim]
    second = widened[..., half_dim:]
    return jnp.concatenate(
        [first * cosine - second * sine, second * cosine + first * sine], axis=-1
    ).astype(jnp.bfloat16)


def join_halves(own_part, other_part):
    even = lax.axis_index("tensor") % 2 == 0
    lower = jnp.where(even, own_part, other_part)
    upper = jnp.where(even, other_part, own_part)
    return jnp.concatenate([lower, upper], axis=-1)


def contract_rows(acts, pieces):
    return tuple((jnp.dot(acts, piece, preferred_element_type=jnp.float32) for piece in pieces))


def body(
    hidden,
    request_of,
    positions,
    page_table,
    attn_gain,
    mlp_gain,
    wq,
    wk,
    wv,
    wo,
    w_gate,
    w_up,
    w_down,
):
    tensor_count = lax.axis_size("tensor")
    rows_dev = hidden.shape[0]
    tok_group = request_of.shape[0]
    query_heads = QH // tensor_count
    key_heads = max(1, KVH // tensor_count)
    group_ratio = QH // KVH
    residual = lax.all_gather(hidden, "tensor", axis=0, tiled=True).astype(jnp.float32)
    normed = rms_scale(residual, attn_gain)
    query_rows = wq.astype(jnp.bfloat16)
    key_rows = wk.astype(jnp.bfloat16)
    value_rows = wv.astype(jnp.bfloat16)
    other_key, other_value = partner((key_rows, value_rows), "tensor", 0)
    key_rows = join_halves(key_rows, other_key)
    value_rows = join_halves(value_rows, other_value)
    query_sum, key_sum, value_sum = contract_rows(
        normed,
        (
            lax.all_gather(query_rows, "group", axis=0, tiled=True),
            lax.all_gather(key_rows, "group", axis=0, tiled=True),
            lax.all_gather(value_rows, "group", axis=0, tiled=True),
        ),
    )
    query_raw = query_sum.astype(jnp.bfloat16)
    key_raw = key_sum.astype(jnp.bfloat16)
    value_raw = value_sum.astype(jnp.bfloat16)
    queries = rotate(query_raw.reshape(tok_group, query_heads, HD), positions)
    keys = rotate(key_raw.reshape(tok_group, key_heads, HD), positions)
    values = value_raw.reshape(tok_group, key_heads, HD)
    kv_rows = jnp.stack([keys, values], axis=2)
    earlier = from_behind(kv_rows, "group", 1)
    earlier_rows = earlier.shape[0]
    all_rows = jnp.concatenate([earlier, kv_rows], axis=0)
    all_keys = jnp.repeat(all_rows[:, :, 0], group_ratio, axis=1)[:, :query_heads]
    all_values = jnp.repeat(all_rows[:, :, 1], group_ratio, axis=1)[:, :query_heads]
    first_request = request_of[0]
    first_position = positions[0]
    same_local = (request_of[:, None] == request_of[None, :]) & (
        positions[None, :] <= positions[:, None]
    )
    same_earlier = (request_of[:, None] == first_request) & (
        jnp.arange(earlier_rows)[None, :] >= earlier_rows - first_position
    )
    visible = jnp.concatenate([same_earlier, same_local], axis=1)
    scores = jnp.einsum(
        "qhd,khd->hqk", queries, all_keys, preferred_element_type=jnp.float32
    ) * HD ** (-0.5)
    scores = jnp.where(visible[None], scores, -1e30)
    row_peak = jnp.max(scores, axis=-1, keepdims=True)
    probs = jnp.where(visible[None], jnp.exp(scores - row_peak), 0.0)
    total = jnp.sum(probs, axis=-1, keepdims=True)
    mixed_heads = jnp.einsum(
        "hqk,khd->qhd", probs.astype(jnp.bfloat16), all_values, preferred_element_type=jnp.float32
    ) / jnp.transpose(total, (1, 0, 2))
    attended = mixed_heads.astype(jnp.bfloat16).reshape(tok_group, query_heads * HD)
    out_rows = wo.astype(jnp.bfloat16)
    attn_part = jnp.dot(
        attended,
        lax.all_gather(out_rows, "group", axis=1, tiled=True),
        preferred_element_type=jnp.float32,
    )
    mixed = residual + lax.psum(attn_part.astype(jnp.bfloat16), "tensor").astype(jnp.float32)
    normed_mlp = rms_scale(mixed, mlp_gain)
    gate_rows = w_gate.astype(jnp.bfloat16)
    up_rows = w_up.astype(jnp.bfloat16)
    gate_sum, up_sum = contract_rows(
        normed_mlp,
        (
            lax.all_gather(gate_rows, "group", axis=0, tiled=True),
            lax.all_gather(up_rows, "group", axis=0, tiled=True),
        ),
    )
    activation = (jax.nn.silu(gate_sum) * up_sum).astype(jnp.bfloat16)
    down_rows = w_down.astype(jnp.bfloat16)
    down_part = jnp.dot(
        activation,
        lax.all_gather(down_rows, "group", axis=1, tiled=True),
        preferred_element_type=jnp.float32,
    )
    summed = lax.psum(down_part.astype(jnp.bfloat16), "tensor").astype(jnp.float32)
    first_row = lax.axis_index("tensor") * rows_dev
    own_mixed = lax.dynamic_slice_in_dim(mixed, first_row, rows_dev, 0)
    own_summed = lax.dynamic_slice_in_dim(summed, first_row, rows_dev, 0)
    layer_out = (own_mixed + own_summed).astype(jnp.bfloat16)
    pages = page_table.shape[1]
    changed = jnp.concatenate(
        [jnp.ones((1,), jnp.int32), (request_of[1:] != request_of[:-1]).astype(jnp.int32)]
    )
    opens = jnp.maximum(changed, (positions % PAGE == 0).astype(jnp.int32))
    logical = jnp.cumsum(opens) - 1
    chosen = jnp.sum(
        jnp.where(logical[:, None] == jnp.arange(pages)[None, :], page_table, 0), axis=1
    )
    target = chosen * PAGE + positions % PAGE
    width = 2 * KVH * HD // tensor_count
    flat_rows = kv_rows.reshape(tok_group, key_heads * 2 * HD)
    offset = lax.axis_index("tensor") * width % (key_heads * 2 * HD)
    own_slice = lax.dynamic_slice_in_dim(flat_rows, offset, width, 1)
    cache = jnp.zeros((pages * PAGE, width), jnp.bfloat16).at[target].set(own_slice)
    return (layer_out, cache.reshape(pages, PAGE, width))


def solution(mesh):
    placed = (
        P(("group", "tensor"), None),
        P("group"),
        P("group"),
        P("group", None),
        P(),
        P(),
        P("group", "tensor"),
        P("group", "tensor"),
        P("group", "tensor"),
        P("tensor", "group"),
        P("group", "tensor"),
        P("group", "tensor"),
        P("tensor", "group"),
    )
    return jax.shard_map(
        body,
        mesh=mesh,
        in_specs=placed,
        out_specs=(P(("group", "tensor"), None), P("group", None, "tensor")),
        check_vma=False,
    )
```

profile of v0, /device:TPU:0, one launch (start us, length us, event | category | flops | bytes accessed | tf_op | source)
XLA Modules:
  0.0 593.4 jit_solution(9900236413319749413)
XLA Ops:
  8.0 0.0 copy-start.8
  8.0 0.0 all-gather.5.cloned.1.call-start
  8.1 0.7 all-gather.5.cloned.1.call-update
  8.8 0.0 all-reduce.3.cloned.1.call-start
  8.8 0.8 convert_element_type.103
  9.6 0.8 convert_element_type.108
  10.5 0.5 collective-permute-start.1
  11.0 0.9 convert_element_type.110
  11.9 1.2 slice.43
  13.1 1.2 slice.42
  14.3 0.8 slice_compare_fusion
  15.2 0.8 maximum_bitcast_fusion
  15.9 0.3 reduce-window.9
  16.2 0.1 slice.57
  16.3 0.9 convert_element_type.117
  17.9 0.1 slice_reduce_fusion
  18.0 0.1 add_bitcast_fusion
  18.1 0.8 select_reduce_fusion
  18.9 1.4 iota_compare_fusion.1
  20.2 0.8 compare_select_fusion
  21.0 30.5 %all_gather.27 = bf16[2048,128]{1,0:T(8,128)(2,1)S(1)} all-gather(bf16[256,128]{1,0:T(8,128)(2,1)S(1)} %convert_element_type.110), channel_id=1, replica_groups=mesh['group'=8,'tensor'=16] {'group'}, dimensions={0}, use_global_device_ids=true | all-gather | bytes 589824 | tf_op jit(solution)/shard_map/all_gather | solution.py:88
  51.6 32.5 %all_gather.28 = bf16[128,2048]{1,0:T(8,128)(2,1)} all-gather(bf16[128,256]{1,0:T(8,128)(2,1)S(1)} %convert_element_type.117), channel_id=1, replica_groups=mesh['group'=8,'tensor'=16] {'group'}, dimensions={1}, use_global_device_ids=true | all-gather | bytes 589824 | tf_op jit(solution)/shard_map/all_gather | solution.py:128
  84.0 3.3 compare_and_fusion
  87.5 29.4 %all_gather.25 = bf16[2048,128]{0,1:T(8,128)(2,1)S(1)} all-gather(bf16[256,128]{0,1:T(8,128)(2,1)S(1)} %pad_maximum_fusion.1), channel_id=1, replica_groups=mesh['group'=8,'tensor'=16] {'group'}, dimensions={0}, use_global_device_ids=true | all-gather | bytes 589824 | tf_op jit(solution)/shard_map/all_gather | solution.py:89
  116.8 30.9 %all_gather.26 = bf16[2048,128]{0,1:T(8,128)(2,1)} all-gather(bf16[256,128]{0,1:T(8,128)(2,1)S(1)} %pad_maximum_fusion.2), channel_id=1, replica_groups=mesh['group'=8,'tensor'=16] {'group'}, dimensions={0}, use_global_device_ids=true | all-gather | bytes 589824 | tf_op jit(solution)/shard_map/all_gather | solution.py:90
  147.7 4.2 fusion.1
  152.0 0.3 copy-done
  152.3 1.5 fusion.3
  153.8 2.2 fusion.13
  156.0 2.2 fusion.16
  158.3 2.2 fusion.14
  160.5 1.7 fusion.52
  162.2 0.1 pad_maximum_fusion
  162.3 4.2 collective-permute-start.2
  166.5 1.5 broadcast_and_fusion
  168.1 7.7 %collective-permute-done.2 = bf16[1536,1,2,128]{0,3,2,1:T(8,128)(2,1)S(1)} collective-permute-done((bf16[1536,1,2,128]{0,3,2,1:T(8,128)(2,1)S(1)}, bf16[1536,1,2,128]{0,3,2,1:T(8,128)(2,1)S(1)}, u32[]{:S(2)}, u32[]{:S(2)}) %collective-permute-start.2) | collective-permute-done | bytes 786464 | tf_op jit(solution)/shard_map/ppermute | solution.py:23
  175.8 0.2 maximum_maximum_fusion
  176.0 0.0 copy-start.3
  176.0 4.1 fusion
  180.1 6.4 %copy-done.1 = f32[1536,3072]{1,0:T(8,128)} copy-done((f32[1536,3072]{1,0:T(8,128)}, f32[1536,3072]{1,0:T(8,128)S(1)}, u32[]{:S(2)}) %copy-start.1) | copy-done | bytes 18874392
  186.5 6.4 %fusion.4 = f32[1536]{0:T(1024)S(1)} fusion(f32[1536,3072]{1,0:T(8,128)S(1)} %get-tuple-element.17, f32[1536]{0:T(1024)S(1)} %get-tuple-element.16, pred[1536,1536]{1,0:T(32,128)(4,1)S(1)} %compare_and_fusion, pred[1536,1536]{1,0:T(32,128)(4,1)S(1)} %broadcast_and_fusion), kind=kLoop, calls=%fused_computation.13 | loop fusion | flops 28310016 | bytes 23605248 | tf_op jit(solution)/shard_map/reduce_sum | solution.py:120
  192.9 14.1 %convolution_convert_fusion.1 = bf16[1536,2048]{1,0:T(8,128)(2,1)} fusion(bf16[128,2048]{1,0:T(8,128)(2,1)} %all_gather.28, f32[1536,3072]{1,0:T(8,128)} %copy-done.1, f32[1536]{0:T(1024)S(1)} %get-tuple-element.16, bf16[3072,1,2,128]{0,3,2,1:T(8,128)(2,1)} %copy-done.3, f32[1536]{0:T(1024)S(1)} %fusion.4, pred[1536,1536]{1,0:T(32,128)(4,1)S(1)} %compare_and_fusion, ...), kind=kOutput, calls=%fused_computation.18 | convolution fusion | flops 2045116416 | bytes 31207424 | tf_op jit(solution)/shard_map/dot_general | solution.py:126
  207.0 0.0 all-reduce.3.cloned.1.call-update
  207.1 0.0 all-gather.7.cloned.1.call-start
  207.1 1.0 copy-done.4
  208.1 0.8 convert_element_type.121
  208.8 0.0 all-gather.7.cloned.1.call-update
  208.8 0.0 all-gather.11.cloned.1.call-start
  208.9 0.7 convert_element_type.124
  209.6 0.0 all-gather.11.cloned.1.call-update
  209.7 0.0 all-gather.9.cloned.1.call-start
  209.7 0.7 convert_element_type.122
  210.5 0.0 all-gather.9.cloned.1.call-update
  210.5 0.0 copy-start.11
  210.5 0.3 all-reduce.5.cloned.1.call-start
  210.8 179.3 %all-reduce.3.cloned.1.call-done = bf16[1536,2048]{1,0:T(8,128)(2,1)} async-done(((bf16[1536,2048]{1,0:T(8,128)(2,1)}), bf16[1536,2048]{1,0:T(8,128)(2,1)}) %all-reduce.3.cloned.1.call-update) | async-done | bytes 6291472 | tf_op jit(solution)/shard_map/psum | solution.py:131
  390.1 11.2 %multiply_reduce_fusion = (f32[1536]{0:T(1024)S(1)}, f32[1536,2048]{1,0:T(8,128)}) fusion(bf16[1536,2048]{1,0:T(8,128)(2,1)} %all-reduce.3.cloned.1.call-done, bf16[1536,2048]{1,0:T(8,128)(2,1)} %all-gather.5.cloned.1.call-done), kind=kLoop, calls=%fused_computation.12 | loop fusion | flops 15727104 | bytes 25171968 | tf_op jit(solution)/shard_map/reduce_sum | solution.py:27
  401.3 10.4 %fusion.64 = f32[1536,512]{1,0:T(8,128)} fusion(bf16[2048,512]{1,0:T(8,128)(2,1)} %all-gather.7.cloned.1.call-done, f32[2048]{0:T(1024)S(1)} %copy-done.11, f32[1536]{0:T(1024)S(1)} %add_rsqrt_fusion, bf16[1536,2048]{1,0:T(8,128)(2,1)} %all-gather.5.cloned.1.call-done, bf16[1536,2048]{1,0:T(8,128)(2,1)} %all-reduce.3.cloned.1.call-done), kind=kOutput, calls=%fused_computation.96 | convolution fusion | flops 3240099840 | bytes 17840128 | tf_op jit(solution)/shard_map/dot_general | solution.py:53
  411.7 15.3 %convolution_convert_fusion = bf16[1536,2048]{1,0:T(8,128)(2,1)} fusion(bf16[512,2048]{1,0:T(8,128)(2,1)} %all-gather.11.cloned.1.call-done, bf16[2048,512]{1,0:T(8,128)(2,1)} %all-gather.9.cloned.1.call-done, f32[1536,512]{1,0:T(8,128)} %fusion.64, f32[2048]{0:T(1024)S(1)} %copy-done.11, f32[1536]{0:T(1024)S(1)} %add_rsqrt_fusion, ...), kind=kOutput, calls=%fused_computation.17 | convolution fusion | flops 6469189632 | bytes 26228736 | tf_op jit(solution)/shard_map/dot_general | solution.py:144
  427.0 0.0 all-reduce.5.cloned.1.call-update
  427.1 0.2 copy.17
  427.3 6.1 %scatter_custom_fusion = bf16[8192,128]{1,0:T(8,128)(2,1)} fusion(s32[1536]{0:T(1024)S(1)} %get-tuple-element.14, bf16[1536,128]{1,0:T(8,128)(2,1)S(1)} %copy.17, bf16[]{:T(256)} %constant.84.clone.1), kind=kCustom, calls=%fused_computation.35 | custom fusion | bytes 2097154 | tf_op jit(solution)/shard_map/scatter | solution.py:168
  433.4 150.6 %all-reduce.5.cloned.1.call-done = bf16[1536,2048]{1,0:T(8,128)(2,1)} async-done(((bf16[1536,2048]{1,0:T(8,128)(2,1)}), bf16[1536,2048]{1,0:T(8,128)(2,1)}) %all-reduce.5.cloned.1.call-update) | async-done | bytes 6291472 | tf_op jit(solution)/shard_map/psum | solution.py:149
  584.0 2.1 add_convert_fusion
  (33 shorter events, 0.2 us)
Async XLA Ops:
  8.0 79.4 %copy-start.9 = (f32[256,64]{0,1:T(8,128)S(1)}, f32[256,64]{0,1:T(8,128)}, u32[]{:S(2)}) copy-start(f32[256,64]{0,1:T(8,128)} %param.20) | copy-start | bytes 196612
  8.0 79.4 %copy-start.8 = (f32[256,64]{0,1:T(8,128)S(1)}, f32[256,64]{0,1:T(8,128)}, u32[]{:S(2)}) copy-start(f32[256,64]{0,1:T(8,128)} %param.21) | copy-start | bytes 196612
  8.0 139.7 %all-gather.5.cloned.1.call-start = ((), (), s32[]{:S(2)}) async-start(), calls=%async_computation | async-start | bytes 6684672 | tf_op jit(solution)/shard_map/all_gather | solution.py:77
  8.8 381.3 %all-reduce.3.cloned.1.call-start = ((), (), s32[]{:S(2)}) async-start(), calls=%async_computation.1 | async-start | bytes 12582912 | tf_op jit(solution)/shard_map/psum | solution.py:131
  9.6 77.7 %collective-permute-start = (bf16[256,64]{0,1:T(8,128)(2,1)S(1)}, bf16[256,64]{0,1:T(8,128)(2,1)S(1)}, u32[]{:S(2)}, u32[]{:S(2)}) collective-permute-start(bf16[256,64]{0,1:T(8,128)(2,1)S(1)} %convert_element_type.103), channel_id=1, source_target_pairs={{0,1},{1,0},{2,3},{3,2},{4,5},{5,4},{6,7},{7,6},{8,9},{9,8},{10,11... | collective-permute-start | bytes 98312 | tf_op jit(solution)/shard_map/ppermute | solution.py:17
  10.5 76.9 %collective-permute-start.1 = (bf16[256,64]{0,1:T(8,128)(2,1)S(1)}, bf16[256,64]{0,1:T(8,128)(2,1)S(1)}, u32[]{:S(2)}, u32[]{:S(2)}) collective-permute-start(bf16[256,64]{0,1:T(8,128)(2,1)S(1)} %convert_element_type.108), channel_id=1, source_target_pairs={{0,1},{1,0},{2,3},{3,2},{4,5},{5,4},{6,7},{7,6},{8,9},{9,8},{10,11... | collective-permute-start | bytes 98312 | tf_op jit(solution)/shard_map/ppermute | solution.py:17
  84.0 67.9 %copy-start.10 = (f32[2048]{0:T(1024)S(1)}, f32[2048]{0:T(1024)}, u32[]{:S(2)}) copy-start(f32[2048]{0:T(1024)} %param.17) | copy-start | bytes 24580
  147.7 4.6 copy-start
  156.0 2.2 copy-start.7
  162.3 13.5 %collective-permute-start.2 = (bf16[1536,1,2,128]{0,3,2,1:T(8,128)(2,1)S(1)}, bf16[1536,1,2,128]{0,3,2,1:T(8,128)(2,1)S(1)}, u32[]{:S(2)}, u32[]{:S(2)}) collective-permute-start(bf16[1536,1,2,128]{0,3,2,1:T(8,128)(2,1)S(1)} %pad_maximum_fusion), channel_id=1, source_target_pairs={{0,16},{16,32},{32,48},{48,64},{64,80},{80,96},{96,112},{1,17},{17... | collective-permute-start | bytes 2359304 | tf_op jit(solution)/shard_map/ppermute | solution.py:23
  168.1 12.0 %copy-start.2 = (pred[1536,1536]{1,0:T(32,128)(4,1)}, pred[1536,1536]{1,0:T(32,128)(4,1)S(1)}, u32[]{:S(2)}) copy-start(pred[1536,1536]{1,0:T(32,128)(4,1)S(1)} %broadcast_and_fusion) | copy-start | bytes 7077892
  176.0 4.1 copy-start.3
  180.1 6.5 %copy-start.1 = (f32[1536,3072]{1,0:T(8,128)}, f32[1536,3072]{1,0:T(8,128)S(1)}, u32[]{:S(2)}) copy-start(f32[1536,3072]{1,0:T(8,128)S(1)} %get-tuple-element.17) | copy-start | bytes 56623108
  207.0 1.0 copy-start.4
  207.0 1.9 copy-start.5
  207.0 2.7 copy-start.6
  207.1 194.2 %all-gather.7.cloned.1.call-start = ((), (), s32[]{:S(2)}) async-start(), calls=%async_computation.2 | async-start | bytes 2359296 | tf_op jit(solution)/shard_map/all_gather | solution.py:138
  208.8 202.8 %all-gather.11.cloned.1.call-start = ((), (), s32[]{:S(2)}) async-start(), calls=%async_computation.4 | async-start | bytes 2359296 | tf_op jit(solution)/shard_map/all_gather | solution.py:146
  209.7 202.0 %all-gather.9.cloned.1.call-start = ((), (), s32[]{:S(2)}) async-start(), calls=%async_computation.3 | async-start | bytes 2359296 | tf_op jit(solution)/shard_map/all_gather | solution.py:139
  210.5 190.8 %copy-start.11 = (f32[2048]{0:T(1024)S(1)}, f32[2048]{0:T(1024)}, u32[]{:S(2)}) copy-start(f32[2048]{0:T(1024)} %param.18) | copy-start | bytes 24580
  210.5 373.5 %all-reduce.5.cloned.1.call-start = ((), (), s32[]{:S(2)}) async-start(), calls=%async_computation.5 | async-start | bytes 12582912 | tf_op jit(solution)/shard_map/psum | solution.py:149
Sparse Core Ops, SparseCore 0:
  11.3 70.2 all-gather.4
  207.2 182.8 all-reduce.2
  427.1 156.8 all-reduce.4
Sparse Core Ops, SparseCore 1:
  209.2 49.1 all-gather.6
  260.3 41.6 all-gather.10
  304.1 50.6 all-gather.8
where the time goes:
time: 594 us; the launch traced here: 593 us
  waiting for transfers between devices  338 us (57%)
  blocking collectives  123 us (21%)
  matrix products  50.5 us (9%)
  other arithmetic  42.9 us (7%)
  local copies, waits for them, and re-layouts  16.7 us (3%)
  between operations  16.4 us (3%)
    psum x1, waiting for transfers between devices, body(): lax.psum(attn_part.astype(jnp.bfloat16), 'tensor').astype(jnp.float32)  179 us
    psum x1, waiting for transfers between devices, body(): lax.psum(down_part.astype(jnp.bfloat16), 'tensor').astype(jnp.float32)  151 us
    all_gather x1, blocking collectives, body(): lax.all_gather(out_rows, 'group', axis=1, tiled=True)  32.5 us
    all_gather x1, blocking collectives, body(): lax.all_gather(value_rows, 'group', axis=0, tiled=True)  30.9 us
    all_gather x1, blocking collectives, body(): lax.all_gather(query_rows, 'group', axis=0, tiled=True)  30.5 us
    all_gather x1, blocking collectives, body(): lax.all_gather(key_rows, 'group', axis=0, tiled=True)  29.4 us
    dot_general x4, matrix products, contract_rows(): jnp.dot(acts, piece, preferred_element_type=jnp.float32)  17 us
    reduce_sum x2, other arithmetic, rms_scale(): square = jnp.mean(values * values, axis=-1, keepdims=True)  15.4 us
  transfers between devices with their start and end apart: 9, of which 3 were waited for; matrix products, arithmetic and copies ran while one was open for 8% of the time, Pallas kernels for 0%

commit v1 on v0

--- a/solution.py
+++ b/solution.py
@@ -128,7 +128,9 @@
         lax.all_gather(out_rows, "group", axis=1, tiled=True),
         preferred_element_type=jnp.float32,
     )
-    mixed = residual + lax.psum(attn_part.astype(jnp.bfloat16), "tensor").astype(jnp.float32)
+    mixed = residual + jnp.sum(
+        lax.all_gather(attn_part.astype(jnp.bfloat16), "tensor"), axis=0
+    ).astype(jnp.float32)
     normed_mlp = rms_scale(mixed, mlp_gain)
     gate_rows = w_gate.astype(jnp.bfloat16)
     up_rows = w_up.astype(jnp.bfloat16)

time: 594 us -> 1020 us (1.72)
  waiting for transfers between devices: 338 us -> 725 us
  other arithmetic: 42.9 us -> 77.9 us
    all_gather x0 -> x1, waiting for transfers between devices: none -> 491 us  [body(): lax.all_gather(attn_part.astype(jnp.bfloat16), 'tensor')]
    psum x1 -> x0, waiting for transfers between devices: 179 us -> none  [body(): lax.psum(attn_part.astype(jnp.bfloat16), 'tensor').astype(jnp.float32)]
    all_gather x1, waiting for transfers between devices: 0.01 us -> 46.2 us  [body(): lax.all_gather(down_rows, 'group', axis=1, tiled=True)]
    reduce_sum x0 -> x1, other arithmetic: none -> 35.1 us  [body(): jnp.sum(lax.all_gather(attn_part.astype(jnp.bfloat16), 'tensor'), axis=0)]
    all_gather x1, waiting for transfers between devices: 0.01 us -> 27.1 us  [body(): lax.all_gather(up_rows, 'group', axis=0, tiled=True)]
  transfers between devices with their start and end apart: 9 -> 9, of which waited for: 3 -> 5; matrix products, arithmetic and copies ran while one was open for 8% -> 8% of each run, Pallas kernels for 0% -> 0%
where the time goes in v1:
time: 1020 us; the launch traced here: 1010 us
  waiting for transfers between devices  725 us (71%)
  blocking collectives  123 us (12%)
  other arithmetic  77.9 us (8%)
  matrix products  50.6 us (5%)
  local copies, waits for them, and re-layouts  16.8 us (2%)
  between operations  15.5 us (2%)
    all_gather x1, waiting for transfers between devices, body(): lax.all_gather(attn_part.astype(jnp.bfloat16), 'tensor')  491 us
    psum x1, waiting for transfers between devices, body(): lax.psum(down_part.astype(jnp.bfloat16), 'tensor').astype(jnp.float32)  152 us
    all_gather x1, waiting for transfers between devices, body(): lax.all_gather(down_rows, 'group', axis=1, tiled=True)  46.2 us
    reduce_sum x1, other arithmetic, body(): jnp.sum(lax.all_gather(attn_part.astype(jnp.bfloat16), 'tensor'), axis=0)  35.1 us
    all_gather x1, blocking collectives, body(): lax.all_gather(out_rows, 'group', axis=1, tiled=True)  32.5 us
    all_gather x1, blocking collectives, body(): lax.all_gather(value_rows, 'group', axis=0, tiled=True)  30.9 us
    all_gather x1, blocking collectives, body(): lax.all_gather(query_rows, 'group', axis=0, tiled=True)  30.5 us
    all_gather x1, blocking collectives, body(): lax.all_gather(key_rows, 'group', axis=0, tiled=True)  29.4 us
  transfers between devices with their start and end apart: 9, of which 5 were waited for; matrix products, arithmetic and copies ran while one was open for 8% of the time, Pallas kernels for 0%

profile of v1, /device:TPU:0, one launch (start us, length us, event | category | flops | bytes accessed | tf_op | source)
XLA Modules:
  0.0 1014.2 jit_solution(1188733496348914486)
XLA Ops:
  7.2 0.0 all-gather.7.cloned.1.call-start
  7.2 0.7 all-gather.7.cloned.1.call-update
  7.9 0.0 all-gather.15.cloned.1.call-start
  8.0 0.8 convert_element_type.105
  8.8 0.8 convert_element_type.110
  9.7 0.5 collective-permute-start.1
  10.2 0.9 convert_element_type.112
  11.1 1.2 slice.43
  12.3 1.2 slice.42
  13.5 0.8 slice_compare_fusion
  14.3 0.8 maximum_bitcast_fusion
  15.1 0.3 reduce-window.9
  15.4 0.1 slice.57
  15.5 0.9 convert_element_type.119
  17.1 0.1 slice_reduce_fusion
  17.2 0.1 add_bitcast_fusion
  17.2 0.8 select_reduce_fusion
  18.0 1.4 iota_compare_fusion.1
  19.4 0.8 compare_select_fusion
  20.2 30.5 %all_gather.33 = bf16[2048,128]{1,0:T(8,128)(2,1)S(1)} all-gather(bf16[256,128]{1,0:T(8,128)(2,1)S(1)} %convert_element_type.112), channel_id=1, replica_groups=mesh['group'=8,'tensor'=16] {'group'}, dimensions={0}, use_global_device_ids=true | all-gather | bytes 589824 | tf_op jit(solution)/shard_map/all_gather | solution.py:88
  50.7 32.5 %all_gather.34 = bf16[128,2048]{1,0:T(8,128)(2,1)} all-gather(bf16[128,256]{1,0:T(8,128)(2,1)S(1)} %convert_element_type.119), channel_id=1, replica_groups=mesh['group'=8,'tensor'=16] {'group'}, dimensions={1}, use_global_device_ids=true | all-gather | bytes 589824 | tf_op jit(solution)/shard_map/all_gather | solution.py:128
  83.2 3.3 compare_and_fusion
  86.7 29.4 %all_gather.31 = bf16[2048,128]{0,1:T(8,128)(2,1)S(1)} all-gather(bf16[256,128]{0,1:T(8,128)(2,1)S(1)} %pad_maximum_fusion.1), channel_id=1, replica_groups=mesh['group'=8,'tensor'=16] {'group'}, dimensions={0}, use_global_device_ids=true | all-gather | bytes 589824 | tf_op jit(solution)/shard_map/all_gather | solution.py:89
  116.0 30.9 %all_gather.32 = bf16[2048,128]{0,1:T(8,128)(2,1)} all-gather(bf16[256,128]{0,1:T(8,128)(2,1)S(1)} %pad_maximum_fusion.2), channel_id=1, replica_groups=mesh['group'=8,'tensor'=16] {'group'}, dimensions={0}, use_global_device_ids=true | all-gather | bytes 589824 | tf_op jit(solution)/shard_map/all_gather | solution.py:90
  146.9 4.2 fusion.1
  151.1 0.3 copy-done
  151.5 1.5 fusion.3
  153.0 2.2 fusion.13
  155.2 2.2 fusion.16
  157.4 2.2 fusion.14
  159.6 1.7 fusion.52
  161.4 0.1 pad_maximum_fusion
  161.5 4.2 collective-permute-start.2
  165.7 1.5 broadcast_and_fusion
  167.3 7.7 collective-permute-done.2
  175.0 0.2 maximum_maximum_fusion
  175.1 4.1 fusion
  179.3 6.4 copy-done.1
  185.7 6.4 fusion.4
  192.1 14.2 %convolution_convert_fusion.1 = bf16[1536,2048]{1,0:T(8,128)(2,1)} fusion(bf16[128,2048]{1,0:T(8,128)(2,1)} %all_gather.34, f32[1536,3072]{1,0:T(8,128)} %copy-done.1, f32[1536]{0:T(1024)S(1)} %get-tuple-element.16, bf16[3072,1,2,128]{0,3,2,1:T(8,128)(2,1)} %copy-done.3, f32[1536]{0:T(1024)S(1)} %fusion.4, pred[1536,1536]{1,0:T(32,128)(4,1)S(1)} %compare_and_fusion, ...), kind=kOutput, calls=%fused_computation.18 | convolution fusion | flops 2045116416 | bytes 31207424 | tf_op jit(solution)/shard_map/dot_general | solution.py:126
  206.3 0.0 all-gather.15.cloned.1.call-update
  206.3 0.0 all-gather.9.cloned.1.call-start
  206.3 1.0 copy-done.4
  207.3 0.7 convert_element_type.123
  208.0 0.0 all-gather.9.cloned.1.call-update
  208.1 0.0 all-gather.11.cloned.1.call-start
  208.1 0.7 convert_element_type.124
  208.9 0.0 all-gather.11.cloned.1.call-update
  208.9 0.0 all-gather.13.cloned.1.call-start
  209.0 0.7 convert_element_type.126
  209.7 0.0 all-gather.13.cloned.1.call-update
  209.7 0.0 all-reduce.2.cloned.1.call-start
  209.8 491.4 %all-gather.15.cloned.1.call-done = bf16[24576,2048]{1,0:T(8,128)(2,1)} async-done(((bf16[1536,2048]{1,0:T(8,128)(2,1)}), bf16[24576,2048]{1,0:T(8,128)(2,1)}) %all-gather.15.cloned.1.call-update) | async-done | bytes 100663312 | tf_op jit(solution)/shard_map/all_gather | solution.py:132
  701.1 35.1 %reduce_sum.50 = bf16[1536,2048]{1,0:T(8,128)(2,1)} reduce(bf16[16,1536,2048]{2,1,0:T(8,128)(2,1)} %bitcast.16, bf16[]{:T(256)} %constant.82.clone.1), dimensions={0}, to_apply=%region_3.4 | reduce | flops 47185920 | bytes 106954752 | tf_op jit(solution)/shard_map/reduce_sum | solution.py:131
  736.2 11.2 %multiply_reduce_fusion = (f32[1536]{0:T(1024)S(1)}, f32[1536,2048]{1,0:T(8,128)}) fusion(bf16[1536,2048]{1,0:T(8,128)(2,1)} %reduce_sum.50, bf16[1536,2048]{1,0:T(8,128)(2,1)} %all-gather.7.cloned.1.call-done), kind=kLoop, calls=%fused_computation.12 | loop fusion | flops 15727104 | bytes 25171968 | tf_op jit(solution)/shard_map/reduce_sum | solution.py:27
  747.4 10.5 %fusion.64 = f32[1536,512]{1,0:T(8,128)} fusion(bf16[2048,512]{1,0:T(8,128)(2,1)} %all-gather.9.cloned.1.call-done, f32[2048]{0:T(1024)S(1)} %copy-done.11, f32[1536]{0:T(1024)S(1)} %add_rsqrt_fusion, bf16[1536,2048]{1,0:T(8,128)(2,1)} %all-gather.7.cloned.1.call-done, bf16[1536,2048]{1,0:T(8,128)(2,1)} %reduce_sum.50), kind=kOutput, calls=%fused_computation.96 | convolution fusion | flops 3240099840 | bytes 17840128 | tf_op jit(solution)/shard_map/dot_general | solution.py:53
  757.9 27.1 %all-gather.11.cloned.1.call-done = bf16[2048,512]{1,0:T(8,128)(2,1)} async-done(((bf16[256,512]{1,0:T(8,128)(2,1)}), bf16[2048,512]{1,0:T(8,128)(2,1)}) %all-gather.11.cloned.1.call-update) | async-done | bytes 2097168 | tf_op jit(solution)/shard_map/all_gather | solution.py:141
  784.9 46.2 %all-gather.13.cloned.1.call-done = bf16[512,2048]{1,0:T(8,128)(2,1)} async-done(((bf16[512,256]{1,0:T(8,128)(2,1)}), bf16[512,2048]{1,0:T(8,128)(2,1)}) %all-gather.13.cloned.1.call-update) | async-done | bytes 2097168 | tf_op jit(solution)/shard_map/all_gather | solution.py:148
  831.2 15.3 %convolution_convert_fusion = bf16[1536,2048]{1,0:T(8,128)(2,1)} fusion(bf16[512,2048]{1,0:T(8,128)(2,1)} %all-gather.13.cloned.1.call-done, bf16[2048,512]{1,0:T(8,128)(2,1)} %all-gather.11.cloned.1.call-done, f32[1536,512]{1,0:T(8,128)} %fusion.64, f32[2048]{0:T(1024)S(1)} %copy-done.11, f32[1536]{0:T(1024)S(1)} %add_rsqrt_fusion, ...), kind=kOutput, calls=%fused_computation.17 | convolution fusion | flops 6469189632 | bytes 26228736 | tf_op jit(solution)/shard_map/dot_general | solution.py:146
  846.5 0.0 all-reduce.2.cloned.1.call-update
  846.6 0.2 copy.17
  846.8 6.1 scatter_custom_fusion
  852.9 152.0 %all-reduce.2.cloned.1.call-done = bf16[1536,2048]{1,0:T(8,128)(2,1)} async-done(((bf16[1536,2048]{1,0:T(8,128)(2,1)}), bf16[1536,2048]{1,0:T(8,128)(2,1)}) %all-reduce.2.cloned.1.call-update) | async-done | bytes 6291472 | tf_op jit(solution)/shard_map/psum | solution.py:151
  1004.9 2.1 add_convert_fusion
  (34 shorter events, 0.2 us)
Async XLA Ops:
  7.2 79.4 %copy-start.9 = (f32[256,64]{0,1:T(8,128)S(1)}, f32[256,64]{0,1:T(8,128)}, u32[]{:S(2)}) copy-start(f32[256,64]{0,1:T(8,128)} %param.20) | copy-start | bytes 196612
  7.2 79.4 %copy-start.8 = (f32[256,64]{0,1:T(8,128)S(1)}, f32[256,64]{0,1:T(8,128)}, u32[]{:S(2)}) copy-start(f32[256,64]{0,1:T(8,128)} %param.21) | copy-start | bytes 196612
  7.2 139.7 %all-gather.7.cloned.1.call-start = ((), (), s32[]{:S(2)}) async-start(), calls=%async_computation | async-start | bytes 6684672 | tf_op jit(solution)/shard_map/all_gather | solution.py:77
  7.9 693.2 %all-gather.15.cloned.1.call-start = ((), (), s32[]{:S(2)}) async-start(), calls=%async_computation.5 | async-start | bytes 106954752 | tf_op jit(solution)/shard_map/all_gather | solution.py:132
  8.8 77.7 %collective-permute-start = (bf16[256,64]{0,1:T(8,128)(2,1)S(1)}, bf16[256,64]{0,1:T(8,128)(2,1)S(1)}, u32[]{:S(2)}, u32[]{:S(2)}) collective-permute-start(bf16[256,64]{0,1:T(8,128)(2,1)S(1)} %convert_element_type.105), channel_id=1, source_target_pairs={{0,1},{1,0},{2,3},{3,2},{4,5},{5,4},{6,7},{7,6},{8,9},{9,8},{10,11... | collective-permute-start | bytes 98312 | tf_op jit(solution)/shard_map/ppermute | solution.py:17
  9.7 76.9 %collective-permute-start.1 = (bf16[256,64]{0,1:T(8,128)(2,1)S(1)}, bf16[256,64]{0,1:T(8,128)(2,1)S(1)}, u32[]{:S(2)}, u32[]{:S(2)}) collective-permute-start(bf16[256,64]{0,1:T(8,128)(2,1)S(1)} %convert_element_type.110), channel_id=1, source_target_pairs={{0,1},{1,0},{2,3},{3,2},{4,5},{5,4},{6,7},{7,6},{8,9},{9,8},{10,11... | collective-permute-start | bytes 98312 | tf_op jit(solution)/shard_map/ppermute | solution.py:17
  83.2 67.9 %copy-start.10 = (f32[2048]{0:T(1024)S(1)}, f32[2048]{0:T(1024)}, u32[]{:S(2)}) copy-start(f32[2048]{0:T(1024)} %param.17) | copy-start | bytes 24580
  146.9 4.6 copy-start
  155.2 2.2 copy-start.7
  161.5 13.5 %collective-permute-start.2 = (bf16[1536,1,2,128]{0,3,2,1:T(8,128)(2,1)S(1)}, bf16[1536,1,2,128]{0,3,2,1:T(8,128)(2,1)S(1)}, u32[]{:S(2)}, u32[]{:S(2)}) collective-permute-start(bf16[1536,1,2,128]{0,3,2,1:T(8,128)(2,1)S(1)} %pad_maximum_fusion), channel_id=1, source_target_pairs={{0,16},{16,32},{32,48},{48,64},{64,80},{80,96},{96,112},{1,17},{17... | collective-permute-start | bytes 2359304 | tf_op jit(solution)/shard_map/ppermute | solution.py:23
  167.2 12.0 %copy-start.2 = (pred[1536,1536]{1,0:T(32,128)(4,1)}, pred[1536,1536]{1,0:T(32,128)(4,1)S(1)}, u32[]{:S(2)}) copy-start(pred[1536,1536]{1,0:T(32,128)(4,1)S(1)} %broadcast_and_fusion) | copy-start | bytes 7077892
  175.1 4.1 copy-start.3
  179.2 6.5 copy-start.1
  206.3 1.0 copy-start.4
  206.3 1.9 copy-start.5
  206.3 2.7 copy-start.6
  206.3 541.1 %all-gather.9.cloned.1.call-start = ((), (), s32[]{:S(2)}) async-start(), calls=%async_computation.1 | async-start | bytes 2359296 | tf_op jit(solution)/shard_map/all_gather | solution.py:140
  208.1 576.8 %all-gather.11.cloned.1.call-start = ((), (), s32[]{:S(2)}) async-start(), calls=%async_computation.2 | async-start | bytes 2359296 | tf_op jit(solution)/shard_map/all_gather | solution.py:141
  208.9 622.3 %all-gather.13.cloned.1.call-start = ((), (), s32[]{:S(2)}) async-start(), calls=%async_computation.3 | async-start | bytes 2359296 | tf_op jit(solution)/shard_map/all_gather | solution.py:148
  209.7 795.2 %all-reduce.2.cloned.1.call-start = ((), (), s32[]{:S(2)}) async-start(), calls=%async_computation.4 | async-start | bytes 12582912 | tf_op jit(solution)/shard_map/psum | solution.py:151
  736.2 11.2 %copy-start.11 = (f32[2048]{0:T(1024)S(1)}, f32[2048]{0:T(1024)}, u32[]{:S(2)}) copy-start(f32[2048]{0:T(1024)} %param.18) | copy-start | bytes 24580
Sparse Core Ops, SparseCore 0:
  10.5 70.2 all-gather.6
  206.4 494.6 all-gather.14
  702.8 39.1 all-gather.8
  744.0 40.8 all-gather.10
  786.9 44.2 all-gather.12
  846.6 158.2 all-reduce.1
